TPU v7x, 32 devices: a whole 2x2x4 slice. The times are simulated.
32 devices in a mesh: groups: 2 (over y), seq: 4 (over z), head: 2 (over x), sub: 2 (over core).
Axes of the slice: x: 2, y: 2, z: 4, core: 2. Of those that a mesh axis runs over, the one named last changes fastest.
Arguments:
- queries: bfloat16 [3072, 8192], P(('groups', 'seq', 'head', 'sub')), parts along dimension 0, may hold values from -128 to 128
- new_keys: bfloat16 [3072, 8192], P(('groups', 'seq', 'head', 'sub')), parts along dimension 0, may hold values from -4 to 4
- new_values: bfloat16 [3072, 8192], P(('groups', 'seq', 'head', 'sub')), parts along dimension 0, may hold values from -6 to 6
- key_cache: bfloat16 [2048, 8192], P(('groups', 'seq'), ('head', 'sub')), parts along dimension 0, may hold values from -6 to 6
- value_cache: bfloat16 [2048, 8192], P(('groups', 'seq'), ('head', 'sub')), parts along dimension 0, may hold values from -6 to 6
- selection: int32 [8, 2], P('groups'), parts along dimension 0, may hold values from 0 to 15, as said below
Outputs:
- attended: bfloat16 [3072, 8192], P(('groups', 'seq', 'head', 'sub')), parts along dimension 0
There are 2 independent parts, one for each index of `groups`. A program takes and returns all parts, laid end to end along the dimension named above; each array names one. Nothing has to cross between parts.
Inputs may be any that keep to these rules, and one draw needn't show every extreme that they name: `selection`: each row names 2 blocks that lie on 2 different indices of seq: the values block // 4 of a row are distinct. Every row names block 15.
All inputs are finite; a program needn't handle non-finite values.
Results may differ from a plain program's by a relative error of at most 0.0033.
Values may be sent and summed in bfloat16 or wider, within the bound.
No kernel may reach another device: no remote copies, remote signals or barrier semaphores. Data moves between devices by JAX's collectives and lax.ppermute only.
A program may use at most 64 MiB of HBM per device.

v0:
```python
import jax
import jax.numpy as jnp
from jax import lax
from jax.sharding import PartitionSpec as P

HD = 128
BLOCK = 64


def split_heads(rows_array, width):
    count = rows_array.shape[0]
    return rows_array.reshape(count, -1, width).transpose(1, 0, 2)


def per_device(queries, new_keys, new_values, key_cache, value_cache, selection):
    q_rows, k_rows, v_rows = (
        lax.all_to_all(queries, ("head", "sub"), split_axis=1, concat_axis=0, tiled=True),
        lax.all_to_all(new_keys, ("head", "sub"), split_axis=1, concat_axis=0, tiled=True),
        lax.all_to_all(new_values, ("head", "sub"), split_axis=1, concat_axis=0, tiled=True),
    )
    width = HD
    scale = float(width) ** (-0.5)
    q_heads = split_heads(q_rows, width)
    k_heads = split_heads(k_rows, width)
    v_heads = split_heads(v_rows, width)
    count = q_rows.shape[0]
    causal = lax.broadcasted_iota(jnp.int32, (count, count), 0) >= lax.broadcasted_iota(
        jnp.int32, (count, count), 1
    )

    def local_scores(pair):
        query_one, key_one = pair
        raw = jnp.dot(query_one, key_one.T, preferred_element_type=jnp.float32) * scale
        return jnp.where(causal, raw, jnp.float32(-1e30))

    me = lax.axis_index("seq")
    blk_dev = key_cache.shape[0] // BLOCK
    owner_of = selection // blk_dev
    matched = owner_of == me
    wanted = jnp.any(matched, axis=1)
    inner = jnp.sum(jnp.where(matched, selection % blk_dev, 0), axis=1)
    cache_k = key_cache.reshape(blk_dev, BLOCK, -1)
    cache_v = value_cache.reshape(blk_dev, BLOCK, -1)
    send_k = jnp.where(wanted[:, None, None], cache_k[inner], jnp.zeros((), jnp.bfloat16))
    send_v = jnp.where(wanted[:, None, None], cache_v[inner], jnp.zeros((), jnp.bfloat16))
    got_k, got_v = (
        lax.all_to_all(send_k, "seq", split_axis=0, concat_axis=0, tiled=True),
        lax.all_to_all(send_v, "seq", split_axis=0, concat_axis=0, tiled=True),
    )
    my_owners = lax.dynamic_index_in_dim(selection, me, 0, keepdims=False) // blk_dev
    fetched_k = split_heads(got_k[my_owners].reshape(-1, got_k.shape[2]), width)
    fetched_v = split_heads(got_v[my_owners].reshape(-1, got_v.shape[2]), width)

    def attend(query_one, value_one, remote_k, remote_v, own_scores):
        remote_scores = jnp.dot(query_one, remote_k.T, preferred_element_type=jnp.float32) * scale
        top = jnp.maximum(
            jnp.max(own_scores, axis=1, keepdims=True),
            jnp.max(remote_scores, axis=1, keepdims=True),
        )
        own_weights = jnp.exp(own_scores - top)
        remote_weights = jnp.exp(remote_scores - top)
        total = jnp.sum(own_weights, axis=1, keepdims=True) + jnp.sum(
            remote_weights, axis=1, keepdims=True
        )
        mixed = jnp.dot(
            own_weights.astype(jnp.bfloat16), value_one, preferred_element_type=jnp.float32
        )
        mixed = mixed + jnp.dot(
            remote_weights.astype(jnp.bfloat16), remote_v, preferred_element_type=jnp.float32
        )
        return (mixed / total).astype(jnp.bfloat16)

    def per_head(items):
        query_one, key_one, value_one, remote_k, remote_v = items
        return attend(query_one, value_one, remote_k, remote_v, local_scores((query_one, key_one)))

    result = lax.map(per_head, (q_heads, k_heads, v_heads, fetched_k, fetched_v))
    joined = result.transpose(1, 0, 2).reshape(count, -1)
    return lax.all_to_all(joined, ("head", "sub"), split_axis=0, concat_axis=1, tiled=True)


def solution(mesh):
    placed = (
        P(("groups", "seq", "head", "sub"), None),
        P(("groups", "seq", "head", "sub"), None),
        P(("groups", "seq", "head", "sub"), None),
        P(("groups", "seq"), ("head", "sub")),
        P(("groups", "seq"), ("head", "sub")),
        P("groups", None),
    )
    return jax.shard_map(
        per_device,
        mesh=mesh,
        in_specs=placed,
        out_specs=P(("groups", "seq", "head", "sub"), None),
        check_vma=False,
    )
```

profile of v0, /device:TPU:0, one launch (start us, length us, event | category | flops | bytes accessed | tf_op | source)
XLA Modules:
  0.0 226.7 jit_solution(10549713549970579454)
XLA Ops:
  0.0 2.8 %copy.40 = bf16[12,4,8,2048]{3,2,0,1:T(8,128)(2,1)} copy(bf16[12,4,8,2048]{3,2,1,0:T(8,128)(2,1)} %bitcast.118) | data formatting | bytes 3145728 | tf_op jit(solution)/shard_map/all_to_all | solution.py:17
  2.8 4.2 %all-to-all-start = ((bf16[96,4,2048]{2,0,1:T(8,128)(2,1)}), bf16[96,4,2048]{2,0,1:T(8,128)(2,1)S(1)}, u32[]{:S(2)}, u32[]{:S(2)}) async-start(bf16[96,4,2048]{2,0,1:T(8,128)(2,1)} %bitcast.109), calls=%async_computation | async-start | bytes 3145728 | tf_op jit(solution)/shard_map/all_to_all | solution.py:17
  7.1 2.7 %copy.39 = bf16[12,4,8,2048]{3,2,0,1:T(8,128)(2,1)} copy(bf16[12,4,8,2048]{3,2,1,0:T(8,128)(2,1)} %bitcast.119) | data formatting | bytes 3145728 | tf_op jit(solution)/shard_map/all_to_all | solution.py:18
  9.8 17.3 %all-to-all-done = bf16[96,4,2048]{2,0,1:T(8,128)(2,1)S(1)} async-done(((bf16[96,4,2048]{2,0,1:T(8,128)(2,1)}), bf16[96,4,2048]{2,0,1:T(8,128)(2,1)S(1)}, u32[]{:S(2)}, u32[]{:S(2)}) %all-to-all-start) | async-done | bytes 1572896 | tf_op jit(solution)/shard_map/all_to_all | solution.py:17
  27.1 4.3 %all-to-all-start.1 = ((bf16[96,4,2048]{2,0,1:T(8,128)(2,1)}), bf16[96,4,2048]{2,0,1:T(8,128)(2,1)}, u32[]{:S(2)}, u32[]{:S(2)}) async-start(bf16[96,4,2048]{2,0,1:T(8,128)(2,1)} %bitcast.108), calls=%async_computation.1 | async-start | bytes 3145728 | tf_op jit(solution)/shard_map/all_to_all | solution.py:18
  31.5 2.7 %copy.38 = bf16[12,4,8,2048]{3,2,0,1:T(8,128)(2,1)} copy(bf16[12,4,8,2048]{3,2,1,0:T(8,128)(2,1)} %bitcast.120) | data formatting | bytes 3145728 | tf_op jit(solution)/shard_map/all_to_all | solution.py:19
  34.2 17.4 %all-to-all-done.1 = bf16[96,4,2048]{2,0,1:T(8,128)(2,1)} async-done(((bf16[96,4,2048]{2,0,1:T(8,128)(2,1)}), bf16[96,4,2048]{2,0,1:T(8,128)(2,1)}, u32[]{:S(2)}, u32[]{:S(2)}) %all-to-all-start.1) | async-done | bytes 1572896 | tf_op jit(solution)/shard_map/all_to_all | solution.py:18
  51.6 4.5 %all-to-all-start.3 = ((bf16[96,4,2048]{2,0,1:T(8,128)(2,1)}), bf16[96,4,2048]{2,0,1:T(8,128)(2,1)}, u32[]{:S(2)}, u32[]{:S(2)}) async-start(bf16[96,4,2048]{2,0,1:T(8,128)(2,1)} %bitcast.107), calls=%async_computation.3 | async-start | bytes 3145728 | tf_op jit(solution)/shard_map/all_to_all | solution.py:19
  56.1 1.6 gather_fusion
  57.7 2.9 %gather_fusion.2 = bf16[4,64,2048]{2,1,0:T(8,128)(2,1)} fusion(bf16[4,64,2048]{2,1,0:T(8,128)(2,1)} %bitcast.121, s32[1024]{0:T(1024)S(1)} %pad_clamp_fusion.1), kind=kCustom, calls=%fused_computation.2 | custom fusion | bytes 2097168 | tf_op jit(solution)/shard_map/gather | solution.py:45
  60.6 3.1 %broadcast_select_fusion = (bf16[4,64,2048]{2,1,0:T(8,128)(2,1)}, bf16[4,64,2048]{2,1,0:T(8,128)(2,1)}) fusion(bf16[4,64,2048]{2,1,0:T(8,128)(2,1)} %gather_fusion.2, pred[4]{0:T(512)(128)(4,1)S(1)} %get-tuple-element.92, bf16[4,64,2048]{2,1,0:T(8,128)(2,1)} %gather_fusion), kind=kLoop, calls=%fused_computation.42 | loop fusion | flops 1048576 | bytes 4194308 | tf_op jit(solution)/shard_map/jit(_where)/select_n | solution.py:45
  63.7 12.5 %all-to-all-done.3 = bf16[96,4,2048]{2,0,1:T(8,128)(2,1)} async-done(((bf16[96,4,2048]{2,0,1:T(8,128)(2,1)}), bf16[96,4,2048]{2,0,1:T(8,128)(2,1)}, u32[]{:S(2)}, u32[]{:S(2)}) %all-to-all-start.3) | async-done | bytes 1572896 | tf_op jit(solution)/shard_map/all_to_all | solution.py:19
  76.2 31.2 %all_to_all.77 = bf16[4,64,2048]{2,1,0:T(8,128)(2,1)} all-to-all(bf16[4,64,2048]{2,1,0:T(8,128)(2,1)} %get-tuple-element.99), channel_id=1, replica_groups=mesh['groups'=2,'seq'=4,'head'=2,'sub'=2] {'seq'}, dimensions={0} | all-to-all | bytes 2097152 | tf_op jit(solution)/shard_map/all_to_all | solution.py:47
  107.3 4.3 %all-to-all-start.4 = ((bf16[4,64,2048]{2,1,0:T(8,128)(2,1)}), bf16[4,64,2048]{2,1,0:T(8,128)(2,1)}, u32[]{:S(2)}, u32[]{:S(2)}) async-start(bf16[4,64,2048]{2,1,0:T(8,128)(2,1)} %get-tuple-element.98), calls=%async_computation.4 | async-start | bytes 2097152 | tf_op jit(solution)/shard_map/all_to_all | solution.py:48
  112.2 1.6 copy.19
  113.8 1.8 copy.31
  115.6 1.6 copy.20
  117.2 1.8 copy.33
  119.4 1.8 gather_fusion.1
  121.3 1.0 copy.21
  122.3 14.1 %all-to-all-done.4 = bf16[4,64,2048]{2,1,0:T(8,128)(2,1)} async-done(((bf16[4,64,2048]{2,1,0:T(8,128)(2,1)}), bf16[4,64,2048]{2,1,0:T(8,128)(2,1)}, u32[]{:S(2)}, u32[]{:S(2)}) %all-to-all-start.4) | async-done | bytes 1048608 | tf_op jit(solution)/shard_map/all_to_all | solution.py:48
  136.4 1.8 gather_fusion.3
  138.5 58.9 %while.11 = (s32[]{:T(128)}, bf16[16,384,128]{2,1,0:T(8,128)(2,1)}, bf16[16,384,128]{2,1,0:T(8,128)(2,1)}, bf16[16,384,128]{2,1,0:T(8,128)(2,1)}, bf16[16,128,12...) while((s32[]{:T(128)}, bf16[16,384,128]{2,1,0:T(8,128)(2,1)}, ...), condition=%wide.region_7.8_spmd.clone, body=%wide.region_2.7_spmd.clone.sunk | while | flops 102284544 | bytes 3337305 | solution.py:77
  138.5 1.2 fusion.55
  139.7 1.1 fusion.56
  142.2 1.2 fusion.55
  143.4 1.1 fusion.56
  145.8 1.2 fusion.55
  147.0 1.1 fusion.56
  148.6 0.9 fusion.60
  149.5 1.2 fusion.55
  150.7 1.1 fusion.56
  153.2 1.2 fusion.55
  154.4 1.1 fusion.56
  156.0 0.9 fusion.60
  156.9 1.2 fusion.55
  158.1 1.1 fusion.56
  160.6 1.2 fusion.55
  161.8 1.1 fusion.56
  163.4 0.9 fusion.60
  164.2 1.2 fusion.55
  165.4 1.1 fusion.56
  167.9 1.2 fusion.55
  169.1 1.1 fusion.56
  170.7 0.9 fusion.60
  171.6 1.2 fusion.55
  172.8 1.1 fusion.56
  175.3 1.2 fusion.55
  176.5 1.1 fusion.56
  178.1 0.9 fusion.60
  179.0 1.2 fusion.55
  180.2 1.1 fusion.56
  182.6 1.2 fusion.55
  183.8 1.1 fusion.56
  186.3 1.2 fusion.55
  187.5 1.1 fusion.56
  190.0 1.2 fusion.55
  191.2 1.1 fusion.56
  193.7 1.2 fusion.55
  194.9 1.1 fusion.56
  197.4 2.4 %copy.24 = bf16[384,16,128]{2,1,0:T(8,128)(2,1)S(1)} copy(bf16[384,16,128]{2,0,1:T(8,128)(2,1)} %bitcast.13) | data formatting | bytes 3145728 | tf_op jit(solution)/shard_map/transpose | solution.py:78
  199.8 2.1 all_to_all.67
  201.8 23.6 %all_to_all.78 = bf16[4,96,2048]{2,1,0:T(8,128)(2,1)S(1)} all-to-all(bf16[4,96,2048]{2,1,0:T(8,128)(2,1)} %all_to_all.67), channel_id=1, replica_groups=mesh['groups'=2,'seq'=4,'head'=2,'sub'=2] {'head','sub'}, dimensions={0} | all-to-all | bytes 3145728 | tf_op jit(solution)/shard_map/all_to_all | solution.py:79
  225.4 1.2 copy.29
  (108 shorter events, 18.7 us)
Async XLA Ops:
  0.0 56.1 %copy-start = (bf16[256,2048]{1,0:T(8,128)(2,1)S(1)}, bf16[256,2048]{1,0:T(8,128)(2,1)}, u32[]{:S(2)}) copy-start(bf16[256,2048]{1,0:T(8,128)(2,1)} %param.11) | copy-start | bytes 3145732
  2.8 24.3 %all-to-all-start = ((bf16[96,4,2048]{2,0,1:T(8,128)(2,1)}), bf16[96,4,2048]{2,0,1:T(8,128)(2,1)S(1)}, u32[]{:S(2)}, u32[]{:S(2)}) async-start(bf16[96,4,2048]{2,0,1:T(8,128)(2,1)} %bitcast.109), calls=%async_computation | async-start | bytes 3145728 | tf_op jit(solution)/shard_map/all_to_all | solution.py:17
  27.1 24.5 %all-to-all-start.1 = ((bf16[96,4,2048]{2,0,1:T(8,128)(2,1)}), bf16[96,4,2048]{2,0,1:T(8,128)(2,1)}, u32[]{:S(2)}, u32[]{:S(2)}) async-start(bf16[96,4,2048]{2,0,1:T(8,128)(2,1)} %bitcast.108), calls=%async_computation.1 | async-start | bytes 3145728 | tf_op jit(solution)/shard_map/all_to_all | solution.py:18
  51.6 4.5 %copy-start.1 = (s32[4,2]{0,1:T(2,128)S(1)}, s32[4,2]{0,1:T(2,128)}, u32[]{:S(2)}) copy-start(s32[4,2]{0,1:T(2,128)} %param.13) | copy-start | bytes 100
  51.6 24.6 %all-to-all-start.3 = ((bf16[96,4,2048]{2,0,1:T(8,128)(2,1)}), bf16[96,4,2048]{2,0,1:T(8,128)(2,1)}, u32[]{:S(2)}, u32[]{:S(2)}) async-start(bf16[96,4,2048]{2,0,1:T(8,128)(2,1)} %bitcast.107), calls=%async_computation.3 | async-start | bytes 3145728 | tf_op jit(solution)/shard_map/all_to_all | solution.py:19
  107.3 29.1 %all-to-all-start.4 = ((bf16[4,64,2048]{2,1,0:T(8,128)(2,1)}), bf16[4,64,2048]{2,1,0:T(8,128)(2,1)}, u32[]{:S(2)}, u32[]{:S(2)}) async-start(bf16[4,64,2048]{2,1,0:T(8,128)(2,1)} %get-tuple-element.98), calls=%async_computation.4 | async-start | bytes 2097152 | tf_op jit(solution)/shard_map/all_to_all | solution.py:48
where the time goes:
time: 229 us; the launch traced here: 227 us
  waiting for transfers between devices  61.3 us (27%)
  matrix products  55.4 us (24%)
  blocking collectives  54.8 us (24%)
  local copies, waits for them, and re-layouts  31.1 us (14%)
  starting transfers between devices  17.3 us (8%)
  other arithmetic  6.25 us (3%)
    all_to_all x1, blocking collectives, per_device(): lax.all_to_all(send_k, 'seq', split_axis=0, concat_axis=0, tiled=True)  31.2 us
    all_to_all x1, blocking collectives, per_device(): lax.all_to_all(joined, ('head', 'sub'), split_axis=0, concat_axis=1, tile...  23.6 us
    dot_general x16, matrix products, local_scores(): jnp.dot(query_one, key_one.T, preferred_element_type=jnp.float32) * scale  19.2 us
    dot_general x16, matrix products, attend(): jnp.dot(query_one, remote_k.T, preferred_element_type=jnp.float32) * scale  17.6 us
    all_to_all x1, waiting for transfers between devices, per_device(): lax.all_to_all(new_keys, ('head', 'sub'), split_axis=1, concat_axis=0, ti...  17.4 us
    all_to_all x1, waiting for transfers between devices, per_device(): lax.all_to_all(queries, ('head', 'sub'), split_axis=1, concat_axis=0, til...  17.3 us
    all_to_all x1, waiting for transfers between devices, per_device(): lax.all_to_all(send_v, 'seq', split_axis=0, concat_axis=0, tiled=True)  14.1 us
    dot_general x16, matrix products, attend(): jnp.dot(remote_weights.astype(jnp.bfloat16), remote_v, preferred_element_...  14 us
  transfers between devices with their start and end apart: 4, of which 4 were waited for; matrix products, arithmetic and copies ran while one was open for 10% of the time, Pallas kernels for 0%

commit v1 on v0

--- a/solution.py
+++ b/solution.py
@@ -16,7 +16,15 @@
     q_rows, k_rows, v_rows = (
         lax.all_to_all(queries, ("head", "sub"), split_axis=1, concat_axis=0, tiled=True),
         lax.all_to_all(new_keys, ("head", "sub"), split_axis=1, concat_axis=0, tiled=True),
-        lax.all_to_all(new_values, ("head", "sub"), split_axis=1, concat_axis=0, tiled=True),
+        jnp.concatenate(
+            lax.all_to_all(
+                jnp.stack(jnp.split(new_values, lax.axis_size(("head", "sub")), axis=1)),
+                ("head", "sub"),
+                0,
+                0,
+            ),
+            axis=0,
+        ),
     )
     width = HD
     scale = float(width) ** (-0.5)

time: 229 us -> 229 us (level)
    all_to_all x1, waiting for transfers between devices: 17.4 us -> 12.5 us  [per_device(): lax.all_to_all(new_keys, ('head', 'sub'), split_axis=1, concat_axis=0, ti...]
    all_to_all x1, waiting for transfers between devices: 12.5 us -> 17.3 us  [per_device(): lax.all_to_all(jnp.stack(jnp.split(new_values, lax.axis_size(('head', 'su...]
    all_to_all x1 -> x0, local copies, waits for them, and re-layouts: 2.73 us -> none  [per_device(): lax.all_to_all(new_values, ('head', 'sub'), split_axis=1, concat_axis=0,...]
where the time goes in v1:
time: 229 us; the launch traced here: 227 us
  waiting for transfers between devices  61.3 us (27%)
  matrix products  55.4 us (24%)
  blocking collectives  54.8 us (24%)
  local copies, waits for them, and re-layouts  29.8 us (13%)
  starting transfers between devices  17.3 us (8%)
  other arithmetic  7.57 us (3%)
    all_to_all x1, blocking collectives, per_device(): lax.all_to_all(send_k, 'seq', split_axis=0, concat_axis=0, tiled=True)  31.2 us
    all_to_all x1, blocking collectives, per_device(): lax.all_to_all(joined, ('head', 'sub'), split_axis=0, concat_axis=1, tile...  23.6 us
    dot_general x16, matrix products, local_scores(): jnp.dot(query_one, key_one.T, preferred_element_type=jnp.float32) * scale  19.2 us
    dot_general x16, matrix products, attend(): jnp.dot(query_one, remote_k.T, preferred_element_type=jnp.float32) * scale  17.6 us
    all_to_all x1, waiting for transfers between devices, per_device(): lax.all_to_all(queries, ('head', 'sub'), split_axis=1, concat_axis=0, til...  17.4 us
    all_to_all x1, waiting for transfers between devices, per_device(): lax.all_to_all(jnp.stack(jnp.split(new_values, lax.axis_size(('head', 'su...  17.3 us
    all_to_all x1, waiting for transfers between devices, per_device(): lax.all_to_all(send_v, 'seq', split_axis=0, concat_axis=0, tiled=True)  14.1 us
    dot_general x16, matrix products, attend(): jnp.dot(remote_weights.astype(jnp.bfloat16), remote_v, preferred_element_...  14 us
  transfers between devices with their start and end apart: 4, of which 4 were waited for; matrix products, arithmetic and copies ran while one was open for 10% of the time, Pallas kernels for 0%

profile of v1, /device:TPU:0, one launch (start us, length us, event | category | flops | bytes accessed | tf_op | source)
XLA Modules:
  0.0 226.8 jit_solution(18228403921981456586)
XLA Ops:
  0.0 1.5 slice_bitcast_fusion.3
  1.6 1.4 pad_maximum_fusion
  2.9 4.2 %all-to-all-start.3 = ((bf16[4,96,2048]{2,1,0:T(8,128)(2,1)}), bf16[4,96,2048]{2,1,0:T(8,128)(2,1)S(1)}, u32[]{:S(2)}, u32[]{:S(2)}) async-start(bf16[4,96,2048]{2,1,0:T(8,128)(2,1)} %pad_maximum_fusion), calls=%async_computation.3 | async-start | bytes 3145728 | tf_op jit(solution)/shard_map/all_to_all | solution.py:20
  7.1 2.7 %copy.35 = bf16[12,4,8,2048]{3,2,0,1:T(8,128)(2,1)} copy(bf16[12,4,8,2048]{3,2,1,0:T(8,128)(2,1)} %bitcast.120) | data formatting | bytes 3145728 | tf_op jit(solution)/shard_map/all_to_all | solution.py:17
  9.9 17.3 %all-to-all-done.3 = bf16[4,96,2048]{2,1,0:T(8,128)(2,1)S(1)} async-done(((bf16[4,96,2048]{2,1,0:T(8,128)(2,1)}), bf16[4,96,2048]{2,1,0:T(8,128)(2,1)S(1)}, u32[]{:S(2)}, u32[]{:S(2)}) %all-to-all-start.3) | async-done | bytes 1572896 | tf_op jit(solution)/shard_map/all_to_all | solution.py:20
  27.2 4.3 %all-to-all-start = ((bf16[96,4,2048]{2,0,1:T(8,128)(2,1)}), bf16[96,4,2048]{2,0,1:T(8,128)(2,1)}, u32[]{:S(2)}, u32[]{:S(2)}) async-start(bf16[96,4,2048]{2,0,1:T(8,128)(2,1)} %bitcast.111), calls=%async_computation | async-start | bytes 3145728 | tf_op jit(solution)/shard_map/all_to_all | solution.py:17
  31.5 2.7 %copy.34 = bf16[12,4,8,2048]{3,2,0,1:T(8,128)(2,1)} copy(bf16[12,4,8,2048]{3,2,1,0:T(8,128)(2,1)} %bitcast.121) | data formatting | bytes 3145728 | tf_op jit(solution)/shard_map/all_to_all | solution.py:18
  34.3 17.4 %all-to-all-done = bf16[96,4,2048]{2,0,1:T(8,128)(2,1)} async-done(((bf16[96,4,2048]{2,0,1:T(8,128)(2,1)}), bf16[96,4,2048]{2,0,1:T(8,128)(2,1)}, u32[]{:S(2)}, u32[]{:S(2)}) %all-to-all-start) | async-done | bytes 1572896 | tf_op jit(solution)/shard_map/all_to_all | solution.py:17
  51.6 4.5 %all-to-all-start.1 = ((bf16[96,4,2048]{2,0,1:T(8,128)(2,1)}), bf16[96,4,2048]{2,0,1:T(8,128)(2,1)}, u32[]{:S(2)}, u32[]{:S(2)}) async-start(bf16[96,4,2048]{2,0,1:T(8,128)(2,1)} %bitcast.110), calls=%async_computation.1 | async-start | bytes 3145728 | tf_op jit(solution)/shard_map/all_to_all | solution.py:18
  56.2 1.6 gather_fusion
  57.8 2.8 %gather_fusion.2 = bf16[4,64,2048]{2,1,0:T(8,128)(2,1)} fusion(bf16[4,64,2048]{2,1,0:T(8,128)(2,1)} %bitcast.122, s32[1024]{0:T(1024)S(1)} %pad_clamp_fusion.1), kind=kCustom, calls=%fused_computation.2 | custom fusion | bytes 2097168 | tf_op jit(solution)/shard_map/gather | solution.py:53
  60.7 3.1 %broadcast_select_fusion = (bf16[4,64,2048]{2,1,0:T(8,128)(2,1)}, bf16[4,64,2048]{2,1,0:T(8,128)(2,1)}) fusion(bf16[4,64,2048]{2,1,0:T(8,128)(2,1)} %gather_fusion.2, pred[4]{0:T(512)(128)(4,1)S(1)} %get-tuple-element.92, bf16[4,64,2048]{2,1,0:T(8,128)(2,1)} %gather_fusion), kind=kLoop, calls=%fused_computation.42 | loop fusion | flops 1048576 | bytes 4194308 | tf_op jit(solution)/shard_map/jit(_where)/select_n | solution.py:53
  63.7 12.5 %all-to-all-done.1 = bf16[96,4,2048]{2,0,1:T(8,128)(2,1)} async-done(((bf16[96,4,2048]{2,0,1:T(8,128)(2,1)}), bf16[96,4,2048]{2,0,1:T(8,128)(2,1)}, u32[]{:S(2)}, u32[]{:S(2)}) %all-to-all-start.1) | async-done | bytes 1572896 | tf_op jit(solution)/shard_map/all_to_all | solution.py:18
  76.2 31.2 %all_to_all.66 = bf16[4,64,2048]{2,1,0:T(8,128)(2,1)} all-to-all(bf16[4,64,2048]{2,1,0:T(8,128)(2,1)} %get-tuple-element.103), channel_id=1, replica_groups=mesh['groups'=2,'seq'=4,'head'=2,'sub'=2] {'seq'}, dimensions={0} | all-to-all | bytes 2097152 | tf_op jit(solution)/shard_map/all_to_all | solution.py:55
  107.4 4.3 %all-to-all-start.4 = ((bf16[4,64,2048]{2,1,0:T(8,128)(2,1)}), bf16[4,64,2048]{2,1,0:T(8,128)(2,1)}, u32[]{:S(2)}, u32[]{:S(2)}) async-start(bf16[4,64,2048]{2,1,0:T(8,128)(2,1)} %get-tuple-element.102), calls=%async_computation.4 | async-start | bytes 2097152 | tf_op jit(solution)/shard_map/all_to_all | solution.py:56
  112.7 1.8 copy.27
  114.6 1.6 copy.17
  116.1 1.8 copy.28
  117.9 1.6 copy.18
  119.5 1.8 gather_fusion.1
  121.4 0.9 copy.19
  122.4 14.1 %all-to-all-done.4 = bf16[4,64,2048]{2,1,0:T(8,128)(2,1)} async-done(((bf16[4,64,2048]{2,1,0:T(8,128)(2,1)}), bf16[4,64,2048]{2,1,0:T(8,128)(2,1)}, u32[]{:S(2)}, u32[]{:S(2)}) %all-to-all-start.4) | async-done | bytes 1048608 | tf_op jit(solution)/shard_map/all_to_all | solution.py:56
  136.5 1.8 gather_fusion.3
  138.6 58.9 %while.11 = (s32[]{:T(128)}, bf16[16,384,128]{2,1,0:T(8,128)(2,1)}, bf16[16,384,128]{2,1,0:T(8,128)(2,1)}, bf16[16,384,128]{2,1,0:T(8,128)(2,1)}, bf16[16,128,12...) while((s32[]{:T(128)}, bf16[16,384,128]{2,1,0:T(8,128)(2,1)}, ...), condition=%wide.region_7.8_spmd.clone, body=%wide.region_2.7_spmd.clone.sunk | while | flops 102284544 | bytes 3337305 | solution.py:85
  138.6 1.2 fusion.55
  139.8 1.1 fusion.56
  142.3 1.2 fusion.55
  143.5 1.1 fusion.56
  145.9 1.2 fusion.55
  147.1 1.1 fusion.56
  149.6 1.2 fusion.55
  150.8 1.1 fusion.56
  153.3 1.2 fusion.55
  154.5 1.1 fusion.56
  157.0 1.2 fusion.55
  158.2 1.1 fusion.56
  159.8 0.9 fusion.60
  160.7 1.2 fusion.55
  161.9 1.1 fusion.56
  164.3 1.2 fusion.55
  165.5 1.1 fusion.56
  167.1 0.9 fusion.60
  168.0 1.2 fusion.55
  169.2 1.1 fusion.56
  171.7 1.2 fusion.55
  172.9 1.1 fusion.56
  174.5 0.9 fusion.60
  175.4 1.2 fusion.55
  176.6 1.1 fusion.56
  179.1 1.2 fusion.55
  180.3 1.1 fusion.56
  181.9 0.9 fusion.60
  182.7 1.2 fusion.55
  183.9 1.1 fusion.56
  186.4 1.2 fusion.55
  187.6 1.1 fusion.56
  190.1 1.2 fusion.55
  191.3 1.1 fusion.56
  193.8 1.2 fusion.55
  195.0 1.1 fusion.56
  197.5 2.4 %copy.22 = bf16[384,16,128]{2,1,0:T(8,128)(2,1)S(1)} copy(bf16[384,16,128]{2,0,1:T(8,128)(2,1)} %bitcast.16) | data formatting | bytes 3145728 | tf_op jit(solution)/shard_map/transpose | solution.py:86
  199.9 2.1 all_to_all.56
  201.9 23.6 %all_to_all.67 = bf16[4,96,2048]{2,1,0:T(8,128)(2,1)S(1)} all-to-all(bf16[4,96,2048]{2,1,0:T(8,128)(2,1)} %all_to_all.56), channel_id=1, replica_groups=mesh['groups'=2,'seq'=4,'head'=2,'sub'=2] {'head','sub'}, dimensions={0} | all-to-all | bytes 3145728 | tf_op jit(solution)/shard_map/all_to_all | solution.py:87
  225.5 1.2 copy.26
  (109 shorter events, 19.6 us)
Async XLA Ops:
  0.0 56.2 %copy-start = (bf16[256,2048]{1,0:T(8,128)(2,1)S(1)}, bf16[256,2048]{1,0:T(8,128)(2,1)}, u32[]{:S(2)}) copy-start(bf16[256,2048]{1,0:T(8,128)(2,1)} %param.11) | copy-start | bytes 3145732
  2.9 24.3 %all-to-all-start.3 = ((bf16[4,96,2048]{2,1,0:T(8,128)(2,1)}), bf16[4,96,2048]{2,1,0:T(8,128)(2,1)S(1)}, u32[]{:S(2)}, u32[]{:S(2)}) async-start(bf16[4,96,2048]{2,1,0:T(8,128)(2,1)} %pad_maximum_fusion), calls=%async_computation.3 | async-start | bytes 3145728 | tf_op jit(solution)/shard_map/all_to_all | solution.py:20
  27.2 24.5 %all-to-all-start = ((bf16[96,4,2048]{2,0,1:T(8,128)(2,1)}), bf16[96,4,2048]{2,0,1:T(8,128)(2,1)}, u32[]{:S(2)}, u32[]{:S(2)}) async-start(bf16[96,4,2048]{2,0,1:T(8,128)(2,1)} %bitcast.111), calls=%async_computation | async-start | bytes 3145728 | tf_op jit(solution)/shard_map/all_to_all | solution.py:17
  51.6 4.5 %copy-start.1 = (s32[4,2]{0,1:T(2,128)S(1)}, s32[4,2]{0,1:T(2,128)}, u32[]{:S(2)}) copy-start(s32[4,2]{0,1:T(2,128)} %param.13) | copy-start | bytes 100
  51.6 24.6 %all-to-all-start.1 = ((bf16[96,4,2048]{2,0,1:T(8,128)(2,1)}), bf16[96,4,2048]{2,0,1:T(8,128)(2,1)}, u32[]{:S(2)}, u32[]{:S(2)}) async-start(bf16[96,4,2048]{2,0,1:T(8,128)(2,1)} %bitcast.110), calls=%async_computation.1 | async-start | bytes 3145728 | tf_op jit(solution)/shard_map/all_to_all | solution.py:18
  107.4 29.1 %all-to-all-start.4 = ((bf16[4,64,2048]{2,1,0:T(8,128)(2,1)}), bf16[4,64,2048]{2,1,0:T(8,128)(2,1)}, u32[]{:S(2)}, u32[]{:S(2)}) async-start(bf16[4,64,2048]{2,1,0:T(8,128)(2,1)} %get-tuple-element.102), calls=%async_computation.4 | async-start | bytes 2097152 | tf_op jit(solution)/shard_map/all_to_all | solution.py:56
